TPU v7x, 32 devices: a whole 2x2x4 slice. The times are simulated.
32 devices in a mesh: groups: 2 (over x), tm: 4 (over y, core), tile: 4 (over z).
Axes of the slice: x: 2, y: 2, z: 4, core: 2. Of those that a mesh axis runs over, the one named last changes fastest.
Arguments:
- activations: float32 [24, 8, 64, 384], P(('groups', 'tm'), 'tile'), parts along dimension 0, may hold values from -200 to 200, as said below
- gain_attention: float32 [384], replicated, may hold values from 0.1 to 1.9
- w_query: float32 [384, 384], replicated, may hold values from -10 to 10, as said below
- w_key: float32 [384, 384], replicated, may hold values from -10 to 10, as said below
- w_value: float32 [384, 384], replicated, may hold values from -0.3125 to 0.3125
- w_out: float32 [384, 384], replicated, may hold values from -0.3125 to 0.3125
- gain_conv: float32 [384], replicated, may hold values from 0.1 to 1.9
- conv_weight: float32 [27, 384, 384], P(None, 'tm'), may hold values from -0.0625 to 0.0625
Outputs:
- attended: float32 [24, 8, 64, 384], P(('groups', 'tm'), 'tile'), parts along dimension 0
- conv_out: float32 [24, 8, 64, 384], P(('groups', 'tm'), 'tile'), parts along dimension 0
There are 2 independent parts, one for each index of `groups`. A program takes and returns all parts, laid end to end along the dimension named above; an argument that names none is the same for every part. Nothing has to cross between parts.
Inputs may be any that keep to these rules, and one draw needn't show every extreme that they name: `activations`: finite latent features. `w_query`: finite projection entries. `w_key`: finite projection entries.
All inputs are finite; a program needn't handle non-finite values.
Results may differ from a plain program's by a relative error of at most 0.00023.
Values sent between devices are 32-bit elements; how exact they have to be, the bound alone decides.
A program may use at most 128 MiB of HBM per device.

v0:
```python
import math

import jax
import jax.numpy as jnp
from jax import lax
from jax.sharding import PartitionSpec as P


def from_behind(block, axis, distance):
    devices = range(lax.axis_size(axis))
    route = [(i - distance, i) for i in devices if i - distance in devices]
    return lax.ppermute(block, axis, route)


def padded_2(x, sides, width):
    for axis, dim in sides:
        size, length = (lax.axis_size(axis), x.shape[dim])
        up = [(i, (i + 1) % size) for i in range(size - 1)]
        down = [(j, i) for i, j in up]
        last = lax.slice_in_dim(x, length - width, length, axis=dim)
        leading = lax.slice_in_dim(x, 0, width, axis=dim)
        before = lax.ppermute(last, axis, up)
        after = lax.ppermute(leading, axis, down)
        x = jnp.concatenate([before, x, after], axis=dim)
    return x


def rms_scale(values, gain):
    return values * lax.rsqrt(jnp.mean(values * values, axis=-1, keepdims=True) + 1e-06) * gain


def tap_columns(source, frame_count, row_count, width_cells):
    pieces = []
    for shift_t in range(3):
        for shift_y in range(3):
            for shift_x in range(3):
                pieces.append(
                    source[
                        ...,
                        shift_t : shift_t + frame_count,
                        shift_y : shift_y + row_count,
                        shift_x : shift_x + width_cells,
                        :,
                    ]
                )
    joined = jnp.concatenate(pieces, axis=-1)
    return joined.reshape(-1, joined.shape[-1])


def body(activations, gain_attention, w_query, w_key, w_value, w_out, gain_conv, conv_weight):
    highest = lax.Precision.HIGHEST
    frame_count, row_count, width_cells, channels = activations.shape
    tokens = row_count * width_cells
    pixels = frame_count * tokens
    scale = 1.0 / math.sqrt(channels)
    normed = rms_scale(activations, gain_attention).reshape(pixels, channels)
    queries = jnp.dot(normed, w_query, precision=highest).reshape(frame_count, tokens, channels)
    key_rows = jnp.dot(normed, w_key, precision=highest).reshape(frame_count, tokens, channels)
    values = jnp.dot(normed, w_value, precision=highest).reshape(frame_count, tokens, channels)
    running = jnp.full((frame_count, tokens), -1e30, jnp.float32)
    key_piece = lax.all_gather(key_rows, "tile", axis=1, tiled=True)
    value_piece = lax.all_gather(values, "tile", axis=1, tiled=True)
    scores = jnp.einsum("fqc,fkc->fqk", queries, key_piece, precision=highest) * scale
    largest = jnp.maximum(running, jnp.max(scores, axis=-1))
    powers = jnp.exp(scores - largest[..., None])
    summed = jnp.sum(powers, axis=-1)
    accumulated = jnp.einsum("fqk,fkc->fqc", powers, value_piece, precision=highest)
    running, summed, accumulated = (largest, summed, accumulated)
    mixed = accumulated / summed[..., None]
    attended = activations + jnp.dot(
        mixed.reshape(pixels, channels), w_out, precision=highest
    ).reshape(activations.shape)
    hidden = jax.nn.silu(rms_scale(attended, gain_conv))
    cached = from_behind(hidden[frame_count - 2 :], "tm", 1)
    stacked = jnp.concatenate([cached, hidden], axis=0)
    padded = padded_2(stacked, (("tile", 1),), 1)
    padded = jnp.pad(padded, ((0, 0), (0, 0), (1, 1), (0, 0)))
    piece = lax.all_gather(conv_weight, "tm", axis=1, tiled=True)
    count = piece.shape[1]
    columns = tap_columns(padded, frame_count, row_count, width_cells)
    conv_out = jnp.dot(columns, piece.reshape(27 * count, channels), precision=highest)
    return (attended, conv_out.reshape(activations.shape))


def solution(mesh):
    return jax.shard_map(
        body,
        mesh=mesh,
        in_specs=(
            P(("groups", "tm"), "tile", None, None),
            P(),
            P(),
            P(),
            P(),
            P(),
            P(),
            P(None, "tm", None),
        ),
        out_specs=(
            P(("groups", "tm"), "tile", None, None),
            P(("groups", "tm"), "tile", None, None),
        ),
        check_vma=False,
    )
```

profile of v0, /device:TPU:0, one launch (start us, length us, event | category | flops | bytes accessed | tf_op | source)
XLA Modules:
  0.0 256.4 jit_solution(7575440983940319005)
XLA Ops:
  7.2 0.0 copy-start
  7.2 0.0 copy-start.1
  7.2 0.0 copy-start.3
  7.2 0.0 all-gather.4.cloned.1.call-start
  7.2 1.3 multiply_reduce_fusion.1
  8.5 1.2 multiply_multiply_fusion
  9.7 3.1 %fusion.8 = f32[3,128,384]{2,1,0:T(8,128)} fusion(f32[3,128,384]{2,1,0:T(8,128)S(1)} %bitcast.33, f32[384,384]{1,0:T(8,128)} %param.11), kind=kOutput, calls=%fused_computation.50 | convolution fusion | flops 679477248 | bytes 1769472 | tf_op jit(solution)/shard_map/dot_general | solution.py:58
  12.9 0.0 all-gather.4.cloned.1.call-update
  12.9 0.0 all-gather.6.cloned.1.call-start
  13.0 3.1 %fusion.6 = f32[3,128,384]{2,1,0:T(8,128)} fusion(f32[3,128,384]{2,1,0:T(8,128)S(1)} %bitcast.34, f32[384,384]{1,0:T(8,128)} %param.12), kind=kOutput, calls=%fused_computation.48 | convolution fusion | flops 679477248 | bytes 1769472 | tf_op jit(solution)/shard_map/dot_general | solution.py:59
  16.1 0.0 all-gather.6.cloned.1.call-update
  16.1 0.0 all-gather.8.cloned.1.call-start
  16.2 0.7 all-gather.8.cloned.1.call-update
  16.9 2.3 fusion.10
  19.2 47.0 %all-gather.4.cloned.1.call-done = f32[3,512,384]{2,1,0:T(8,128)} async-done(((f32[3,128,384]{2,1,0:T(8,128)}), f32[3,512,384]{2,1,0:T(8,128)}) %all-gather.4.cloned.1.call-update) | async-done | bytes 2359312 | tf_op jit(solution)/shard_map/all_gather | solution.py:61
  66.2 4.3 %fusion.15 = (f32[3,128]{1,0:T(4,128)S(1)}, f32[3,128,512]{2,1,0:T(8,128)S(1)}) fusion(f32[3,128,384]{2,1,0:T(8,128)S(1)} %fusion.10, f32[3,512,384]{2,1,0:T(8,128)} %all-gather.4.cloned.1.call-done), kind=kOutput, calls=%fused_computation.65 | convolution fusion | flops 906362496 | bytes 3737088 | tf_op jit(solution)/shard_map/fqc,fkc->fqk/dot_general | solution.py:63
  70.5 0.3 fusion.1
  70.8 46.9 %all-gather.6.cloned.1.call-done = f32[3,512,384]{2,1,0:T(8,128)} async-done(((f32[3,128,384]{2,1,0:T(8,128)}), f32[3,512,384]{2,1,0:T(8,128)}) %all-gather.6.cloned.1.call-update) | async-done | bytes 2359312 | tf_op jit(solution)/shard_map/all_gather | solution.py:62
  117.7 3.5 %convolution_divide_fusion = f32[3,128,384]{2,1,0:T(8,128)S(1)} fusion(f32[3,512,384]{2,1,0:T(8,128)} %all-gather.6.cloned.1.call-done, f32[3,128,512]{2,1,0:T(8,128)S(1)} %get-tuple-element.7, f32[3,128]{1,0:T(4,128)S(1)} %broadcast_maximum_fusion, f32[3,128]{1,0:T(4,128)S(1)} %fusion.1), kind=kOutput, calls=%fused_computation.16 | convolution fusion | flops 906313728 | bytes 3738624 | tf_op jit(solution)/shard_map/fqk,fkc->fqc/dot_general | solution.py:67
  121.2 0.0 copy-done
  121.2 0.0 copy-done.1
  121.2 1.4 multiply_reduce_fusion
  122.6 0.0 copy-start.2
  122.6 0.0 copy-done.3
  122.7 0.2 divide_multiply_fusion
  122.9 1.8 collective-permute-start
  124.7 1.3 collective-permute-done
  126.0 0.1 fusion.12
  126.1 1.6 collective-permute-start.1
  127.7 1.5 collective-permute-start.2
  129.2 4.8 %collective-permute-done.1 = f32[5,1,64,384]{3,2,1,0:T(8,128)S(1)} collective-permute-done((f32[5,1,64,384]{3,2,1,0:T(8,128)S(1)}, f32[5,1,64,384]{3,2,1,0:T(8,128)S(1)}, u32[]{:S(2)}, u32[]{:S(2)}) %collective-permute-start.1) | collective-permute-done | bytes 491552 | tf_op jit(solution)/shard_map/ppermute | solution.py:22
  134.0 4.5 %collective-permute-done.2 = f32[5,1,64,384]{3,2,1,0:T(8,128)S(1)} collective-permute-done((f32[5,1,64,384]{3,2,1,0:T(8,128)S(1)}, f32[5,1,64,384]{3,2,1,0:T(8,128)S(1)}, u32[]{:S(2)}, u32[]{:S(2)}) %collective-permute-start.2) | collective-permute-done | bytes 491552 | tf_op jit(solution)/shard_map/ppermute | solution.py:23
  138.5 0.4 pad_maximum_fusion
  138.9 0.2 select_maximum_fusion
  139.2 0.9 slice_dynamic-update-slice_fusion.23
  140.0 0.9 slice_dynamic-update-slice_fusion.22
  141.0 0.9 slice_dynamic-update-slice_fusion.21
  141.9 0.9 slice_dynamic-update-slice_fusion.20
  142.8 0.9 fusion.3
  143.7 1.0 slice_dynamic-update-slice_fusion.19
  144.7 0.9 slice_dynamic-update-slice_fusion.18
  145.6 0.9 slice_dynamic-update-slice_fusion.17
  146.5 0.9 slice_dynamic-update-slice_fusion.16
  147.4 0.9 slice_dynamic-update-slice_fusion.15
  148.3 0.9 slice_dynamic-update-slice_fusion.14
  149.2 0.9 slice_dynamic-update-slice_fusion.13
  150.1 0.9 slice_dynamic-update-slice_fusion.12
  151.0 0.9 fusion.4
  151.9 0.9 slice_dynamic-update-slice_fusion.11
  152.9 0.9 slice_dynamic-update-slice_fusion.10
  153.8 0.9 slice_dynamic-update-slice_fusion.9
  154.7 0.9 slice_dynamic-update-slice_fusion.8
  155.6 0.9 slice_dynamic-update-slice_fusion.7
  156.5 0.9 slice_dynamic-update-slice_fusion.6
  157.4 0.9 slice_dynamic-update-slice_fusion.5
  158.4 0.9 slice_dynamic-update-slice_fusion.4
  159.2 0.0 copy-done.2
  159.2 1.1 constant_dynamic-update-slice_fusion
  160.4 0.9 slice_dynamic-update-slice_fusion.3
  161.3 1.0 slice_dynamic-update-slice_fusion.2
  162.3 0.9 slice_dynamic-update-slice_fusion.1
  163.1 0.9 slice_dynamic-update-slice_fusion
  164.0 55.2 %all-gather.8.cloned.1.call-done = f32[27,384,384]{2,1,0:T(8,128)} async-done(((f32[27,96,384]{2,1,0:T(8,128)}), f32[27,384,384]{2,1,0:T(8,128)}) %all-gather.8.cloned.1.call-update) | async-done | bytes 15925264 | tf_op jit(solution)/shard_map/all_gather | solution.py:78
  219.2 30.7 %fusion.16 = f32[3,2,64,384]{3,2,1,0:T(8,128)} fusion(f32[3,2,64,10368]{3,2,1,0:T(8,128)} %slice_dynamic-update-slice_fusion, f32[10368,384,1,1]{1,0,3,2:T(8,128)} %bitcast.32), kind=kOutput, calls=%fused_computation.66 | convolution fusion | flops 18345885696 | bytes 32440320 | tf_op jit(solution)/shard_map/dot_general | solution.py:81
  (4 shorter events, 0.0 us)
Async XLA Ops:
  7.2 114.0 %copy-start = (f32[384,384]{1,0:T(8,128)S(1)}, f32[384,384]{1,0:T(8,128)}, u32[]{:S(2)}) copy-start(f32[384,384]{1,0:T(8,128)} %param.13) | copy-start | bytes 1769476
  7.2 114.0 %copy-start.1 = (f32[3,2,64,384]{3,2,1,0:T(8,128)S(1)}, f32[3,2,64,384]{3,2,1,0:T(8,128)}, u32[]{:S(2)}) copy-start(f32[3,2,64,384]{3,2,1,0:T(8,128)} %param.8) | copy-start | bytes 1769476
  7.2 115.5 %copy-start.3 = (f32[384]{0:T(512)S(1)}, f32[384]{0:T(512)}, u32[]{:S(2)}) copy-start(f32[384]{0:T(512)} %param.14) | copy-start | bytes 4612
  7.2 59.0 %all-gather.4.cloned.1.call-start = ((), (), s32[]{:S(2)}) async-start(), calls=%async_computation | async-start | bytes 2949120 | tf_op jit(solution)/shard_map/all_gather | solution.py:61
  12.9 104.8 %all-gather.6.cloned.1.call-start = ((), (), s32[]{:S(2)}) async-start(), calls=%async_computation.1 | async-start | bytes 2949120 | tf_op jit(solution)/shard_map/all_gather | solution.py:62
  16.1 203.1 %all-gather.8.cloned.1.call-start = ((), (), s32[]{:S(2)}) async-start(), calls=%async_computation.2 | async-start | bytes 19906560 | tf_op jit(solution)/shard_map/all_gather | solution.py:78
  122.6 36.6 %copy-start.2 = (f32[3,2,64,384]{3,2,1,0:T(8,128)}, f32[3,2,64,384]{3,2,1,0:T(8,128)S(1)}, u32[]{:S(2)}) copy-start(f32[3,2,64,384]{3,2,1,0:T(8,128)S(1)} %get-tuple-element.9) | copy-start | bytes 1769476
  122.9 3.1 %collective-permute-start = (f32[2,2,64,384]{3,2,1,0:T(8,128)S(1)}, f32[2,2,64,384]{3,2,1,0:T(8,128)S(1)}, u32[]{:S(2)}, u32[]{:S(2)}) collective-permute-start(f32[2,2,64,384]{3,2,1,0:T(8,128)S(1)} %slice.135), channel_id=1, source_target_pairs={{0,4},{4,8},{8,12},{1,5},{5,9},{9,13},{2,6},{6,10},{10,14},{3,7},{... | collective-permute-start | bytes 1179656 | tf_op jit(solution)/shard_map/ppermute | solution.py:12
  126.1 8.0 %collective-permute-start.1 = (f32[5,1,64,384]{3,2,1,0:T(8,128)S(1)}, f32[5,1,64,384]{3,2,1,0:T(8,128)S(1)}, u32[]{:S(2)}, u32[]{:S(2)}) collective-permute-start(f32[5,1,64,384]{3,2,1,0:T(8,128)S(1)} %get-tuple-element.4), channel_id=1, source_target_pairs={{0,1},{1,2},{2,3},{4,5},{5,6},{6,7},{8,9},{9,10},{10,11},{12,13},{... | collective-permute-start | bytes 1474568 | tf_op jit(solution)/shard_map/ppermute | solution.py:22
  127.7 10.8 %collective-permute-start.2 = (f32[5,1,64,384]{3,2,1,0:T(8,128)S(1)}, f32[5,1,64,384]{3,2,1,0:T(8,128)S(1)}, u32[]{:S(2)}, u32[]{:S(2)}) collective-permute-start(f32[5,1,64,384]{3,2,1,0:T(8,128)S(1)} %get-tuple-element.5), channel_id=1, source_target_pairs={{1,0},{2,1},{3,2},{5,4},{6,5},{7,6},{9,8},{10,9},{11,10},{13,12},{... | collective-permute-start | bytes 1474568 | tf_op jit(solution)/shard_map/ppermute | solution.py:23
Sparse Core Ops, SparseCore 0:
  13.0 53.1 all-gather.3
  68.3 49.2 all-gather.5
  119.2 99.9 all-gather.7
where the time goes:
time: 257 us; the launch traced here: 256 us
  waiting for transfers between devices  160 us (62%)
  matrix products  48.5 us (19%)
  local copies, waits for them, and re-layouts  22 us (9%)
  between operations  13.9 us (5%)
  other arithmetic  6.63 us (3%)
  starting transfers between devices  5 us (2%)
    all_gather x1, waiting for transfers between devices, body(): piece = lax.all_gather(conv_weight, 'tm', axis=1, tiled=True)  55.2 us
    all_gather x1, waiting for transfers between devices, body(): key_piece = lax.all_gather(key_rows, 'tile', axis=1, tiled=True)  47 us
    all_gather x1, waiting for transfers between devices, body(): value_piece = lax.all_gather(values, 'tile', axis=1, tiled=True)  46.9 us
    dot_general x1, matrix products, body(): jnp.dot(columns, piece.reshape(27 * count, channels), precision=highest)  30.7 us
    unnamed x31, local copies, waits for them, and re-layouts  21 us
  transfers between devices with their start and end apart: 6, of which 6 were waited for; matrix products, arithmetic and copies ran while one was open for 16% of the time, Pallas kernels for 0%

commit v1 on v0

v1 whole, which is shorter than its diff:
```python
import functools
import math

import jax
import jax.numpy as jnp
from jax import lax
from jax.experimental import pallas as pl
from jax.experimental.pallas import tpu as pltpu
from jax.sharding import PartitionSpec as P

F32, BF16 = jnp.float32, jnp.bfloat16
VMEM_LIMIT = 56 * 1024 * 1024
CHUNKS = 3


def split(x):
    high = x.astype(BF16)
    return high, (x - high.astype(F32)).astype(BF16)


def dot3(a, b, dims=(((1,), (0,)), ((), ()))):
    dot = functools.partial(lax.dot_general, dimension_numbers=dims, preferred_element_type=F32)
    (ah, al), (bh, bl) = a, b
    return dot(ah, bh) + (dot(ah, bl) + dot(al, bh))


TRANSPOSED = (((1,), (1,)), ((), ()))


def rms(v, gain):
    return v * lax.rsqrt(jnp.mean(v * v, axis=-1, keepdims=True) + 1e-06) * gain


def attention_kernel(slots, position, own, *refs):
    lefts, rights = refs[:slots], refs[slots : 2 * slots]
    gain_a, wq, wk, wv, wo, gain_c, attended, hidden = refs[2 * slots :]
    me = position[0]
    gain = gain_a[...]
    x = own[...]
    normed = split(rms(x, gain))
    queries = dot3(normed, split(wq[...]))
    folded = split(dot3(split(queries), split(wk[...]), TRANSPOSED))
    scale = 1.0 / math.sqrt(x.shape[-1])
    cells = [normed]
    for s in range(1, slots + 1):
        block = jnp.where(me >= s, lefts[s - 1][...], rights[slots - s][...])
        cells.append(split(rms(block, gain)))
    keys = tuple(jnp.concatenate([c[i] for c in cells], axis=0) for i in range(2))
    scores = dot3(folded, keys, TRANSPOSED) * scale
    powers = jnp.exp(scores - jnp.max(scores, axis=-1, keepdims=True))
    summed = jnp.sum(powers, axis=-1, keepdims=True)
    gathered = dot3(split(powers), keys) / summed
    mixed = dot3(split(gathered), split(wv[...]))
    result = x + dot3(split(mixed), split(wo[...]))
    attended[...] = result
    v = rms(result, gain_c[...])
    hidden[...] = v / (1.0 + jnp.exp(-v))


def attention(position, own, lefts, rights, gain_a, wq, wk, wv, wo, gain_c):
    frames, tokens, channels = own.shape
    block = pl.BlockSpec((None, tokens, channels), lambda f, p: (f, 0, 0))
    gain = pl.BlockSpec((1, channels), lambda f, p: (0, 0))
    weight = pl.BlockSpec((channels, channels), lambda f, p: (0, 0))
    slots = len(lefts)
    shape = jax.ShapeDtypeStruct(own.shape, F32)
    return pl.pallas_call(
        functools.partial(attention_kernel, slots),
        grid_spec=pltpu.PrefetchScalarGridSpec(
            num_scalar_prefetch=1,
            grid=(frames,),
            in_specs=[block] * (1 + 2 * slots) + [gain] + [weight] * 4 + [gain],
            out_specs=[block, block],
        ),
        out_shape=[shape, shape],
        cost_estimate=pl.CostEstimate(flops=3 * 10**9, bytes_accessed=10**7, transcendentals=10**6),
        compiler_params=pltpu.CompilerParams(vmem_limit_bytes=VMEM_LIMIT),
    )(position, own, *lefts, *rights, gain_a.reshape(1, -1), wq, wk, wv, wo, gain_c.reshape(1, -1))


def conv_kernel(sizes, offsets, hidden, up, down, past, past_up, past_down, *refs):
    slots = len(sizes)
    shards = [refs[c * slots : (c + 1) * slots] for c in range(CHUNKS)]
    out, xh, xl, stage, wh, wl = refs[CHUNKS * slots :]
    frames, rows, width, channels = hidden.shape
    step = pl.program_id(0)

    @pl.when(step == 0)
    def _():
        cell = lax.broadcasted_iota(jnp.int32, (width, channels), 0)
        for f in range(frames + 2):
            for r in range(rows + 2):
                upper, middle, lower, t = (past_up, past, past_down, f) if f < 2 else (up, hidden, down, f - 2)
                if r == 0:
                    value = upper[t, 0]
                elif r == rows + 1:
                    value = lower[t, 0]
                else:
                    value = middle[t, r - 1]
                before = jnp.where(cell == 0, 0.0, pltpu.roll(value, 1, 0))
                after = jnp.where(cell == width - 1, 0.0, pltpu.roll(value, width - 1, 0))
                for c, v in enumerate((before, value, after)):
                    high, low = split(v)
                    xh[f, r, :, c * channels : (c + 1) * channels] = high
                    xl[f, r, :, c * channels : (c + 1) * channels] = low
        out[...] = jnp.zeros_like(out)

    direct = all(s % 16 == 0 for s in sizes)
    for chunk in range(CHUNKS):

        @pl.when(step // 3 == chunk)
        def _(chunk=chunk):
            for slot, size in enumerate(sizes):
                unit = math.gcd(*sizes)
                for c in range(3):
                    row = pl.multiple_of(c * channels + offsets[slot], unit)
                    value = shards[chunk][slot][c]
                    if direct:
                        high, low = split(value)
                        wh[pl.ds(row, size)] = high
                        wl[pl.ds(row, size)] = low
                    else:
                        stage[pl.ds(row, size)] = value

    if not direct:
        high, low = split(stage[...])
        wh[...] = high
        wl[...] = low
    a, b = step // 3, step % 3
    pixels = frames * rows * width
    left = xh[pl.ds(a, frames), pl.ds(b, rows)].reshape(pixels, 3 * channels)
    left_low = xl[pl.ds(a, frames), pl.ds(b, rows)].reshape(pixels, 3 * channels)
    out[...] += dot3((left, left_low), (wh[...], wl[...]))


def conv(offsets, halo, shards):
    hidden = halo[0]
    frames, rows, width, channels = hidden.shape
    sizes = tuple(s.shape[1] for s in shards[0])
    pixels = frames * rows * width
    whole = [pl.BlockSpec(h.shape, lambda g, o: (0, 0, 0, 0)) for h in halo]
    parts = []
    for chunk in range(CHUNKS):
        for size in sizes:
            parts.append(
                pl.BlockSpec(
                    (3, size, channels),
                    lambda g, o, chunk=chunk: (jnp.clip(g - 3 * chunk, 0, 2), 0, 0),
                )
            )
    direct = all(s % 16 == 0 for s in sizes)
    return pl.pallas_call(
        functools.partial(conv_kernel, sizes),
        grid_spec=pltpu.PrefetchScalarGridSpec(
            num_scalar_prefetch=1,
            grid=(9,),
            in_specs=whole + parts,
            out_specs=pl.BlockSpec((pixels, channels), lambda g, o: (0, 0)),
            scratch_shapes=[
                pltpu.VMEM((frames + 2, rows + 2, width, 3 * channels), BF16),
                pltpu.VMEM((frames + 2, rows + 2, width, 3 * channels), BF16),
                pltpu.VMEM((8 if direct else 3 * channels, channels), F32),
                pltpu.VMEM((3 * channels, channels), BF16),
                pltpu.VMEM((3 * channels, channels), BF16),
            ],
        ),
        out_shape=jax.ShapeDtypeStruct((pixels, channels), F32),
        cost_estimate=pl.CostEstimate(flops=9 * 10**9, bytes_accessed=2 * 10**7, transcendentals=0),
        compiler_params=pltpu.CompilerParams(vmem_limit_bytes=VMEM_LIMIT),
    )(offsets, *halo, *[s for chunk in shards for s in chunk])


def exchange(x, axis, bit):
    return lax.ppermute(x, axis, [(i, i ^ bit) for i in range(lax.axis_size(axis))])


def kernel_shards(conv_weight):
    shards, groups = lax.axis_size("tm"), lax.axis_size("groups")
    me, group = lax.axis_index("tm"), lax.axis_index("groups")
    size = conv_weight.shape[1]
    taps = conv_weight.shape[0] // CHUNKS
    pieces = [conv_weight[c * taps : (c + 1) * taps] for c in range(CHUNKS)]
    halved = groups == 2 and size % 32 == 0
    half = size // 2
    chunks = []
    for piece in pieces:
        slots, offsets = [piece], [me * size]
        far = 1
        while 2 * far < shards:
            far *= 2
        held = [(0, 0, piece)]
        bit = far
        while bit >= 1:
            arrived = []
            for mask, kind, array in held:
                if halved and bit > 1 and kind == 0:
                    mine = lax.dynamic_slice_in_dim(array, group * half, half, axis=1)
                    first = exchange(mine, "tm", bit)
                    second = exchange(first, "groups", 1)
                    arrived += [(mask ^ bit, 1, first), (mask ^ bit, 2, second)]
                else:
                    arrived.append((mask ^ bit, kind, exchange(array, "tm", bit)))
            held += arrived
            bit //= 2
        chunks.append([array for _, _, array in held])
    starts = {0: 0, 1: group * half, 2: (1 - group) * half}
    offsets = jnp.stack([(me ^ mask) * size + starts[kind] for mask, kind, _ in held])
    return offsets.astype(jnp.int32), chunks


def line_gather(x, axis):
    size = lax.axis_size(axis)
    up = [(i, i + 1) for i in range(size - 1)]
    down = [(i + 1, i) for i in range(size - 1)]
    lefts, rights = [], []
    left = right = x
    for _ in range(size - 1):
        left = lax.ppermute(left, axis, up)
        right = lax.ppermute(right, axis, down)
        lefts.append(left)
        rights.append(right)
    return lefts, rights


def shifted(x, frame_step, tile_step):
    times, tiles = lax.axis_size("tm"), lax.axis_size("tile")
    route = []
    for t in range(times):
        for z in range(tiles):
            if t + frame_step < times and 0 <= z + tile_step < tiles:
                route.append((t * tiles + z, (t + frame_step) * tiles + z + tile_step))
    return lax.ppermute(x, ("tm", "tile"), route)


def body(activations, gain_attention, w_query, w_key, w_value, w_out, gain_conv, conv_weight):
    frames, rows, width, channels = activations.shape
    own = activations.reshape(frames, rows * width, channels)
    lefts, rights = line_gather(own, "tile")
    offsets, shards = kernel_shards(conv_weight)
    position = lax.axis_index("tile").reshape(1).astype(jnp.int32)
    attended, hidden = attention(
        position, own, lefts, rights, gain_attention, w_query, w_key, w_value, w_out, gain_conv
    )
    hidden = hidden.reshape(activations.shape)
    last = hidden[frames - 2 :]
    halo = (
        hidden,
        shifted(hidden[:, rows - 1 :], 0, 1),
        shifted(hidden[:, :1], 0, -1),
        shifted(last, 1, 0),
        shifted(last[:, rows - 1 :], 1, 1),
        shifted(last[:, :1], 1, -1),
    )
    conv_out = conv(offsets, halo, shards)
    return (attended.reshape(activations.shape), conv_out.reshape(activations.shape))


def solution(mesh):
    placed = P(("groups", "tm"), "tile", None, None)
    return jax.shard_map(
        body,
        mesh=mesh,
        in_specs=(placed, P(), P(), P(), P(), P(), P(), P(None, "tm", None)),
        out_specs=(placed, placed),
        check_vma=False,
    )
```

time: 257 us -> 152 us (0.59)
  the two profiles are of different devices: /device:TPU:0 before, /device:TPU:11 now
where the time goes in v1:
time: 152 us; the launch traced here: 151 us
  waiting for transfers between devices  56.6 us (37%)
  starting transfers between devices  45.8 us (30%)
  Pallas kernels  34.1 us (22%)
  local copies, waits for them, and re-layouts  13.8 us (9%)
    ppermute x15, waiting for transfers between devices, exchange(): lax.ppermute(x, axis, [(i, i ^ bit) for i in range(lax.axis_size(axis))])  38.2 us
    pallas_call x1, Pallas kernels, conv(): pl.pallas_call(functools.partial(conv_kernel, sizes), grid_spec=pltpu.Pre...  23.6 us
    ppermute x15, starting transfers between devices, exchange(): lax.ppermute(x, axis, [(i, i ^ bit) for i in range(lax.axis_size(axis))])  15.6 us
    ppermute x5, starting transfers between devices, shifted(): return lax.ppermute(x, ('tm', 'tile'), route)  14.4 us
    ppermute x5, waiting for transfers between devices, shifted(): return lax.ppermute(x, ('tm', 'tile'), route)  14.1 us
    pallas_call x1, Pallas kernels, attention(): pl.pallas_call(functools.partial(attention_kernel, slots), grid_spec=pltp...  10.5 us
    ppermute x3, starting transfers between devices, line_gather(): left = lax.ppermute(left, axis, up)  9.06 us
    ppermute x3, starting transfers between devices, line_gather(): right = lax.ppermute(right, axis, down)  6.77 us
  transfers between devices with their start and end apart: 26, of which 10 were waited for; matrix products, arithmetic and copies ran while one was open for 7% of the time, Pallas kernels for 7%

profile of v1, /device:TPU:11, one launch (start us, length us, event | category | flops | bytes accessed | tf_op | source)
XLA Modules:
  0.0 151.2 jit_solution(4931674583651850453)
XLA Ops:
  0.6 2.1 %collective-permute-start.3 = (f32[3,128,384]{2,1,0:T(8,128)}, f32[3,128,384]{2,1,0:T(8,128)S(1)}, u32[]{:S(2)}, u32[]{:S(2)}) collective-permute-start(f32[3,128,384]{2,1,0:T(8,128)} %bitcast.14), channel_id=1, source_target_pairs={{1,0},{2,1},{3,2},{5,4},{6,5},{7,6},{9,8},{10,9},{11,10},{13,12},{... | collective-permute-start | bytes 1769480 | tf_op jit(solution)/shard_map/ppermute | solution.py:219
  2.7 3.2 %collective-permute-start = (f32[3,128,384]{2,1,0:T(8,128)}, f32[3,128,384]{2,1,0:T(8,128)}, u32[]{:S(2)}, u32[]{:S(2)}) collective-permute-start(f32[3,128,384]{2,1,0:T(8,128)} %bitcast.15), channel_id=1, source_target_pairs={{0,1},{1,2},{2,3},{4,5},{5,6},{6,7},{8,9},{9,10},{10,11},{12,13},{... | collective-permute-start | bytes 1769480 | tf_op jit(solution)/shard_map/ppermute | solution.py:218
  5.9 3.5 %fusion = (f32[9,96,384]{2,1,0:T(8,128)S(1)}, f32[9,96,384]{2,1,0:T(8,128)S(1)}, f32[9,96,384]{2,1,0:T(8,128)}) fusion(f32[27,96,384]{2,1,0:T(8,128)} %param.15), kind=kLoop, calls=%fused_computation.3 | loop fusion | bytes 7962624 | tf_op jit(solution)/shard_map/slice | solution.py:182
  9.4 1.6 %constant_dynamic-slice_fusion.1 = f32[9,48,384]{2,1,0:T(8,128)S(1)} fusion(f32[9,96,384]{2,1,0:T(8,128)} %get-tuple-element.8.refs_6_, s32[]{:T(128)S(6)} %select_n.2), kind=kLoop, calls=%fused_computation.1 | loop fusion | bytes 1327108 | tf_op jit(solution)/shard_map/dynamic_slice | solution.py:197
  11.1 1.3 collective-permute-start.16
  12.4 0.3 collective-permute-start.11
  12.7 1.3 collective-permute-start.21
  14.1 3.0 %collective-permute-done.3.refs_3_ = f32[3,128,384]{2,1,0:T(8,128)S(1)} collective-permute-done((f32[3,128,384]{2,1,0:T(8,128)}, f32[3,128,384]{2,1,0:T(8,128)S(1)}, u32[]{:S(2)}, u32[]{:S(2)}) %collective-permute-start.3) | collective-permute-done | bytes 589856 | tf_op jit(solution)/shard_map/ppermute | solution.py:219
  17.0 2.0 %collective-permute-start.4 = (f32[3,128,384]{2,1,0:T(8,128)S(1)}, f32[3,128,384]{2,1,0:T(8,128)S(1)}, u32[]{:S(2)}, u32[]{:S(2)}) collective-permute-start(f32[3,128,384]{2,1,0:T(8,128)S(1)} %collective-permute-done.3.refs_3_), channel_id=1, source_target_pairs={{1,0},{2,1},{3,2},{5,4},{6,5},{7,6},{9,8},{10,9},{11,10},{13,12},{... | collective-permute-start | bytes 1769480 | tf_op jit(solution)/shard_map/ppermute | solution.py:219
  19.0 0.0 collective-permute-done.refs_0_
  19.0 3.3 %collective-permute-start.1 = (f32[3,128,384]{2,1,0:T(8,128)}, f32[3,128,384]{2,1,0:T(8,128)S(1)}, u32[]{:S(2)}, u32[]{:S(2)}) collective-permute-start(f32[3,128,384]{2,1,0:T(8,128)} %collective-permute-done.refs_0_), channel_id=1, source_target_pairs={{0,1},{1,2},{2,3},{4,5},{5,6},{6,7},{8,9},{9,10},{10,11},{12,13},{... | collective-permute-start | bytes 1769480 | tf_op jit(solution)/shard_map/ppermute | solution.py:218
  22.3 3.9 %collective-permute-done.16.refs_7_ = f32[9,48,384]{2,1,0:T(8,128)S(1)} collective-permute-done((f32[9,48,384]{2,1,0:T(8,128)S(1)}, f32[9,48,384]{2,1,0:T(8,128)S(1)}, u32[]{:S(2)}, u32[]{:S(2)}) %collective-permute-start.16) | collective-permute-done | bytes 663584 | tf_op jit(solution)/shard_map/ppermute | solution.py:174
  26.3 3.9 %collective-permute-start.19 = (f32[9,48,384]{2,1,0:T(8,128)S(1)}, f32[9,48,384]{2,1,0:T(8,128)S(1)}, u32[]{:S(2)}, u32[]{:S(2)}) collective-permute-start(f32[9,48,384]{2,1,0:T(8,128)S(1)} %collective-permute-done.16.refs_7_), channel_id=1, source_target_pairs={{0,4},{4,0},{8,12},{12,8},{1,5},{5,1},{9,13},{13,9},{2,6},{6,2},{1... | collective-permute-start | bytes 1990664 | tf_op jit(solution)/shard_map/ppermute | solution.py:174
  30.2 10.3 %collective-permute-done.11.refs_1_ = f32[9,48,384]{2,1,0:T(8,128)S(1)} collective-permute-done((f32[9,48,384]{2,1,0:T(8,128)S(1)}, f32[9,48,384]{2,1,0:T(8,128)S(1)}, u32[]{:S(2)}, u32[]{:S(2)}) %collective-permute-start.11) | collective-permute-done | bytes 663584 | tf_op jit(solution)/shard_map/ppermute | solution.py:174
  40.5 0.3 collective-permute-start.17
  40.8 14.1 %collective-permute-done.21.refs_13_ = f32[9,48,384]{2,1,0:T(8,128)} collective-permute-done((f32[9,48,384]{2,1,0:T(8,128)S(1)}, f32[9,48,384]{2,1,0:T(8,128)}, u32[]{:S(2)}, u32[]{:S(2)}) %collective-permute-start.21) | collective-permute-done | bytes 663584 | tf_op jit(solution)/shard_map/ppermute | solution.py:174
  54.8 2.2 %collective-permute-start.14 = (f32[9,48,384]{2,1,0:T(8,128)S(1)}, f32[9,48,384]{2,1,0:T(8,128)S(1)}, u32[]{:S(2)}, u32[]{:S(2)}) collective-permute-start(f32[9,48,384]{2,1,0:T(8,128)S(1)} %collective-permute-done.11.refs_1_), channel_id=1, source_target_pairs={{0,4},{4,0},{8,12},{12,8},{1,5},{5,1},{9,13},{13,9},{2,6},{6,2},{1... | collective-permute-start | bytes 1990664 | tf_op jit(solution)/shard_map/ppermute | solution.py:174
  57.0 0.0 collective-permute-done.4.refs_4_
  57.0 0.3 collective-permute-start.12
  57.2 0.0 collective-permute-done.1.refs_1_
  57.3 2.7 %collective-permute-start.5 = (f32[3,128,384]{2,1,0:T(8,128)S(1)}, f32[3,128,384]{2,1,0:T(8,128)S(1)}, u32[]{:S(2)}, u32[]{:S(2)}) collective-permute-start(f32[3,128,384]{2,1,0:T(8,128)S(1)} %collective-permute-done.4.refs_4_), channel_id=1, source_target_pairs={{1,0},{2,1},{3,2},{5,4},{6,5},{7,6},{9,8},{10,9},{11,10},{13,12},{... | collective-permute-start | bytes 1769480 | tf_op jit(solution)/shard_map/ppermute | solution.py:219
  60.0 0.0 collective-permute-done.19.refs_10_
  60.0 2.5 %collective-permute-start.2 = (f32[3,128,384]{2,1,0:T(8,128)S(1)}, f32[3,128,384]{2,1,0:T(8,128)S(1)}, u32[]{:S(2)}, u32[]{:S(2)}) collective-permute-start(f32[3,128,384]{2,1,0:T(8,128)S(1)} %collective-permute-done.1.refs_1_), channel_id=1, source_target_pairs={{0,1},{1,2},{2,3},{4,5},{5,6},{6,7},{8,9},{9,10},{10,11},{12,13},{... | collective-permute-start | bytes 1769480 | tf_op jit(solution)/shard_map/ppermute | solution.py:218
  62.6 0.0 collective-permute-done.17.refs_8_
  62.6 1.0 collective-permute-start.23
  63.6 0.0 collective-permute-done.14.refs_4_
  63.6 0.1 collective-permute-start.13
  63.7 9.9 %collective-permute-done.12.refs_2_ = f32[9,48,384]{2,1,0:T(8,128)} collective-permute-done((f32[9,48,384]{2,1,0:T(8,128)S(1)}, f32[9,48,384]{2,1,0:T(8,128)}, u32[]{:S(2)}, u32[]{:S(2)}) %collective-permute-start.12) | collective-permute-done | bytes 663584 | tf_op jit(solution)/shard_map/ppermute | solution.py:174
  73.6 0.9 collective-permute-start.18
  74.4 0.0 collective-permute-done.5.refs_5_
  74.4 0.4 collective-permute-start.24
  74.9 1.3 collective-permute-done.2.refs_2_
  76.2 0.8 copy-done.18
  77.0 1.4 collective-permute-start.22
  78.4 0.6 reshape.28.refs_6_
  79.0 0.6 reshape.29.refs_11_
  79.6 10.5 %shard_map.95 = (f32[3,128,384]{2,1,0:T(8,128)}, f32[3,128,384]{2,1,0:T(8,128)}) custom-call(s32[1]{0:T(128)} %bitcast.position, f32[3,128,384]{2,1,0:T(8,128)} %bitcast.16, f32[3,128,384]{2,1,0:T(8,128)} %collective-permute-done.refs_0_, f32[3,128,384]{2,1,0:T(8,128)} %copy-done.16, f32[3,128,384]{2,1,0:T(8,128)} %copy-done.18, f32[3,128,384]{2,1,0:T(8,128)} %copy-done.14, ...), custom_call_target="tpu_custom_call" | custom-call | flops 3000000000 | bytes 10000000 | tf_op jit(solution)/shard_map/pallas_call | solution.py:67
  90.1 1.8 %slice.29 = f32[2,128,384]{2,1,0:T(8,128)} slice(f32[3,128,384]{2,1,0:T(8,128)} %get-tuple-element.5), slice={[1:3], [0:128], [0:384]} | slice | bytes 786432 | tf_op jit(solution)/shard_map/slice | solution.py:245
  92.0 0.0 collective-permute-done.24.refs_16_
  92.0 1.8 %collective-permute-start.20 = (f32[9,48,384]{2,1,0:T(8,128)S(1)}, f32[9,48,384]{2,1,0:T(8,128)S(1)}, u32[]{:S(2)}, u32[]{:S(2)}) collective-permute-start(f32[9,48,384]{2,1,0:T(8,128)S(1)} %copy-done.9), channel_id=1, source_target_pairs={{0,4},{4,0},{8,12},{12,8},{1,5},{5,1},{9,13},{13,9},{2,6},{6,2},{1... | collective-permute-start | bytes 1990664 | tf_op jit(solution)/shard_map/ppermute | solution.py:174
  93.7 1.0 fusion.2
  94.8 0.0 collective-permute-done.22.refs_14_
  94.8 2.7 %collective-permute-start.10 = (f32[2,1,64,384]{3,2,1,0:T(8,128)S(1)}, f32[2,1,64,384]{3,2,1,0:T(8,128)S(1)}, u32[]{:S(2)}, u32[]{:S(2)}) collective-permute-start(f32[2,1,64,384]{3,2,1,0:T(8,128)S(1)} %get-tuple-element.11), channel_id=1, source_target_pairs={{1,4},{2,5},{3,6},{5,8},{6,9},{7,10},{9,12},{10,13},{11,14},{17,20... | collective-permute-start | bytes 589832 | tf_op jit(solution)/shard_map/ppermute | solution.py:232
  97.5 0.0 collective-permute-done.23.refs_15_
  97.5 0.1 collective-permute-start.15
  97.6 0.0 collective-permute-done.13.refs_3_
  97.6 0.5 collective-permute-start.25
  98.1 0.0 collective-permute-done.18.refs_9_
  98.1 2.3 %collective-permute-start.8 = (f32[2,2,64,384]{3,2,1,0:T(8,128)}, f32[2,2,64,384]{3,2,1,0:T(8,128)S(1)}, u32[]{:S(2)}, u32[]{:S(2)}) collective-permute-start(f32[2,2,64,384]{3,2,1,0:T(8,128)} %bitcast.10), channel_id=1, source_target_pairs={{0,4},{1,5},{2,6},{3,7},{4,8},{5,9},{6,10},{7,11},{8,12},{9,13},{1... | collective-permute-start | bytes 1179656 | tf_op jit(solution)/shard_map/ppermute | solution.py:232
  100.4 3.3 %collective-permute-done.10.past_down = f32[2,1,64,384]{3,2,1,0:T(8,128)S(1)} collective-permute-done((f32[2,1,64,384]{3,2,1,0:T(8,128)S(1)}, f32[2,1,64,384]{3,2,1,0:T(8,128)S(1)}, u32[]{:S(2)}, u32[]{:S(2)}) %collective-permute-start.10) | collective-permute-done | bytes 196640 | tf_op jit(solution)/shard_map/ppermute | solution.py:232
  103.6 4.2 %collective-permute-start.9 = (f32[2,1,64,384]{3,2,1,0:T(8,128)S(1)}, f32[2,1,64,384]{3,2,1,0:T(8,128)S(1)}, u32[]{:S(2)}, u32[]{:S(2)}) collective-permute-start(f32[2,1,64,384]{3,2,1,0:T(8,128)S(1)} %get-tuple-element.12), channel_id=1, source_target_pairs={{0,5},{1,6},{2,7},{4,9},{5,10},{6,11},{8,13},{9,14},{10,15},{16,21... | collective-permute-start | bytes 589832 | tf_op jit(solution)/shard_map/ppermute | solution.py:232
  107.9 3.5 %collective-permute-done.9.past_up = f32[2,1,64,384]{3,2,1,0:T(8,128)S(1)} collective-permute-done((f32[2,1,64,384]{3,2,1,0:T(8,128)S(1)}, f32[2,1,64,384]{3,2,1,0:T(8,128)S(1)}, u32[]{:S(2)}, u32[]{:S(2)}) %collective-permute-start.9) | collective-permute-done | bytes 196640 | tf_op jit(solution)/shard_map/ppermute | solution.py:232
  111.4 0.7 copy-done.23
  112.1 2.8 %collective-permute-start.7 = (f32[3,1,64,384]{3,2,1,0:T(8,128)S(1)}, f32[3,1,64,384]{3,2,1,0:T(8,128)S(1)}, u32[]{:S(2)}, u32[]{:S(2)}) collective-permute-start(f32[3,1,64,384]{3,2,1,0:T(8,128)S(1)} %get-tuple-element.9), channel_id=1, source_target_pairs={{1,0},{2,1},{3,2},{5,4},{6,5},{7,6},{9,8},{10,9},{11,10},{13,12},{... | collective-permute-start | bytes 884744 | tf_op jit(solution)/shard_map/ppermute | solution.py:232
  114.9 0.8 copy-done.11
  115.7 2.5 %collective-permute-start.6 = (f32[3,1,64,384]{3,2,1,0:T(8,128)S(1)}, f32[3,1,64,384]{3,2,1,0:T(8,128)S(1)}, u32[]{:S(2)}, u32[]{:S(2)}) collective-permute-start(f32[3,1,64,384]{3,2,1,0:T(8,128)S(1)} %get-tuple-element.10), channel_id=1, source_target_pairs={{0,1},{1,2},{2,3},{4,5},{5,6},{6,7},{8,9},{9,10},{10,11},{12,13},{... | collective-permute-start | bytes 884744 | tf_op jit(solution)/shard_map/ppermute | solution.py:232
  118.2 0.6 stack.27.offsets
  118.8 0.0 collective-permute-done.15.refs_5_
  118.8 0.0 collective-permute-done.25.refs_17_
  118.9 3.5 %collective-permute-done.7.down = f32[3,1,64,384]{3,2,1,0:T(8,128)S(1)} collective-permute-done((f32[3,1,64,384]{3,2,1,0:T(8,128)S(1)}, f32[3,1,64,384]{3,2,1,0:T(8,128)S(1)}, u32[]{:S(2)}, u32[]{:S(2)}) %collective-permute-start.7) | collective-permute-done | bytes 294944 | tf_op jit(solution)/shard_map/ppermute | solution.py:232
  122.4 3.9 %collective-permute-done.6.up = f32[3,1,64,384]{3,2,1,0:T(8,128)S(1)} collective-permute-done((f32[3,1,64,384]{3,2,1,0:T(8,128)S(1)}, f32[3,1,64,384]{3,2,1,0:T(8,128)S(1)}, u32[]{:S(2)}, u32[]{:S(2)}) %collective-permute-start.6) | collective-permute-done | bytes 294944 | tf_op jit(solution)/shard_map/ppermute | solution.py:232
  126.3 0.7 copy-done.21
  126.9 0.7 copy-done.19
  127.7 23.6 %shard_map.96 = f32[384,384]{1,0:T(8,128)} custom-call(s32[6]{0:T(128)} %stack.27.offsets, f32[3,2,64,384]{3,2,1,0:T(8,128)} %bitcast.12, f32[3,1,64,384]{3,2,1,0:T(8,128)} %copy-done.21, f32[3,1,64,384]{3,2,1,0:T(8,128)} %copy-done.20, f32[2,2,64,384]{3,2,1,0:T(8,128)} %copy-done.19, f32[2,1,64,384]{3,2,1,0:T(8,128)} %copy-done.23, ...), custom_call_target="tpu_custom_call" | custom-call | flops 8999999488 | bytes 20000000 | tf_op jit(solution)/shard_map/pallas_call | solution.py:152
  (48 shorter events, 0.2 us)
Async XLA Ops:
  0.6 16.4 %collective-permute-start.3 = (f32[3,128,384]{2,1,0:T(8,128)}, f32[3,128,384]{2,1,0:T(8,128)S(1)}, u32[]{:S(2)}, u32[]{:S(2)}) collective-permute-start(f32[3,128,384]{2,1,0:T(8,128)} %bitcast.14), channel_id=1, source_target_pairs={{1,0},{2,1},{3,2},{5,4},{6,5},{7,6},{9,8},{10,9},{11,10},{13,12},{... | collective-permute-start | bytes 1769480 | tf_op jit(solution)/shard_map/ppermute | solution.py:219
  2.7 16.3 %collective-permute-start = (f32[3,128,384]{2,1,0:T(8,128)}, f32[3,128,384]{2,1,0:T(8,128)}, u32[]{:S(2)}, u32[]{:S(2)}) collective-permute-start(f32[3,128,384]{2,1,0:T(8,128)} %bitcast.15), channel_id=1, source_target_pairs={{0,1},{1,2},{2,3},{4,5},{5,6},{6,7},{8,9},{9,10},{10,11},{12,13},{... | collective-permute-start | bytes 1769480 | tf_op jit(solution)/shard_map/ppermute | solution.py:218
  9.4 53.1 %copy-start = (f32[9,96,384]{2,1,0:T(8,128)}, f32[9,96,384]{2,1,0:T(8,128)S(1)}, u32[]{:S(2)}) copy-start(f32[9,96,384]{2,1,0:T(8,128)S(1)} %get-tuple-element.6.refs_12_) | copy-start | bytes 3981316
  9.4 54.1 %copy-start.1 = (f32[9,96,384]{2,1,0:T(8,128)}, f32[9,96,384]{2,1,0:T(8,128)S(1)}, u32[]{:S(2)}) copy-start(f32[9,96,384]{2,1,0:T(8,128)S(1)} %get-tuple-element.7.refs_0_) | copy-start | bytes 3981316
  11.1 15.2 %collective-permute-start.16 = (f32[9,48,384]{2,1,0:T(8,128)S(1)}, f32[9,48,384]{2,1,0:T(8,128)S(1)}, u32[]{:S(2)}, u32[]{:S(2)}) collective-permute-start(f32[9,48,384]{2,1,0:T(8,128)S(1)} %constant_dynamic-slice_fusion.1), channel_id=1, source_target_pairs={{0,8},{4,12},{8,0},{12,4},{1,9},{5,13},{9,1},{13,5},{2,10},{6,14},... | collective-permute-start | bytes 1990664 | tf_op jit(solution)/shard_map/ppermute | solution.py:174
  12.4 66.0 %copy-start.3 = (f32[384]{0:T(512)S(1)}, f32[384]{0:T(512)}, u32[]{:S(2)}) copy-start(f32[384]{0:T(512)} %param.9) | copy-start | bytes 4612
  12.4 66.6 %copy-start.4 = (f32[384]{0:T(512)S(1)}, f32[384]{0:T(512)}, u32[]{:S(2)}) copy-start(f32[384]{0:T(512)} %param.14) | copy-start | bytes 4612
  12.4 28.1 %collective-permute-start.11 = (f32[9,48,384]{2,1,0:T(8,128)S(1)}, f32[9,48,384]{2,1,0:T(8,128)S(1)}, u32[]{:S(2)}, u32[]{:S(2)}) collective-permute-start(f32[9,48,384]{2,1,0:T(8,128)S(1)} %constant_dynamic-slice_fusion.2), channel_id=1, source_target_pairs={{0,8},{4,12},{8,0},{12,4},{1,9},{5,13},{9,1},{13,5},{2,10},{6,14},... | collective-permute-start | bytes 1990664 | tf_op jit(solution)/shard_map/ppermute | solution.py:174
  12.7 42.1 %collective-permute-start.21 = (f32[9,48,384]{2,1,0:T(8,128)S(1)}, f32[9,48,384]{2,1,0:T(8,128)}, u32[]{:S(2)}, u32[]{:S(2)}) collective-permute-start(f32[9,48,384]{2,1,0:T(8,128)S(1)} %constant_dynamic-slice_fusion), channel_id=1, source_target_pairs={{0,8},{4,12},{8,0},{12,4},{1,9},{5,13},{9,1},{13,5},{2,10},{6,14},... | collective-permute-start | bytes 1990664 | tf_op jit(solution)/shard_map/ppermute | solution.py:174
  17.0 62.5 %copy-start.14 = (f32[3,128,384]{2,1,0:T(8,128)}, f32[3,128,384]{2,1,0:T(8,128)S(1)}, u32[]{:S(2)}) copy-start(f32[3,128,384]{2,1,0:T(8,128)S(1)} %collective-permute-done.3.refs_3_) | copy-start | bytes 1769476
  17.0 39.9 %collective-permute-start.4 = (f32[3,128,384]{2,1,0:T(8,128)S(1)}, f32[3,128,384]{2,1,0:T(8,128)S(1)}, u32[]{:S(2)}, u32[]{:S(2)}) collective-permute-start(f32[3,128,384]{2,1,0:T(8,128)S(1)} %collective-permute-done.3.refs_3_), channel_id=1, source_target_pairs={{1,0},{2,1},{3,2},{5,4},{6,5},{7,6},{9,8},{10,9},{11,10},{13,12},{... | collective-permute-start | bytes 1769480 | tf_op jit(solution)/shard_map/ppermute | solution.py:219
  19.0 38.2 %collective-permute-start.1 = (f32[3,128,384]{2,1,0:T(8,128)}, f32[3,128,384]{2,1,0:T(8,128)S(1)}, u32[]{:S(2)}, u32[]{:S(2)}) collective-permute-start(f32[3,128,384]{2,1,0:T(8,128)} %collective-permute-done.refs_0_), channel_id=1, source_target_pairs={{0,1},{1,2},{2,3},{4,5},{5,6},{6,7},{8,9},{9,10},{10,11},{12,13},{... | collective-permute-start | bytes 1769480 | tf_op jit(solution)/shard_map/ppermute | solution.py:218
  26.3 37.4 %copy-start.5 = (f32[9,48,384]{2,1,0:T(8,128)}, f32[9,48,384]{2,1,0:T(8,128)S(1)}, u32[]{:S(2)}) copy-start(f32[9,48,384]{2,1,0:T(8,128)S(1)} %collective-permute-done.16.refs_7_) | copy-start | bytes 1990660
  26.3 33.7 %collective-permute-start.19 = (f32[9,48,384]{2,1,0:T(8,128)S(1)}, f32[9,48,384]{2,1,0:T(8,128)S(1)}, u32[]{:S(2)}, u32[]{:S(2)}) collective-permute-start(f32[9,48,384]{2,1,0:T(8,128)S(1)} %collective-permute-done.16.refs_7_), channel_id=1, source_target_pairs={{0,4},{4,0},{8,12},{12,8},{1,5},{5,1},{9,13},{13,9},{2,6},{6,2},{1... | collective-permute-start | bytes 1990664 | tf_op jit(solution)/shard_map/ppermute | solution.py:174
  40.5 33.1 %copy-start.6 = (f32[9,48,384]{2,1,0:T(8,128)}, f32[9,48,384]{2,1,0:T(8,128)S(1)}, u32[]{:S(2)}) copy-start(f32[9,48,384]{2,1,0:T(8,128)S(1)} %collective-permute-done.11.refs_1_) | copy-start | bytes 1990660
  40.5 22.1 %collective-permute-start.17 = (f32[9,48,384]{2,1,0:T(8,128)S(1)}, f32[9,48,384]{2,1,0:T(8,128)S(1)}, u32[]{:S(2)}, u32[]{:S(2)}) collective-permute-start(f32[9,48,384]{2,1,0:T(8,128)S(1)} %collective-permute-done.16.refs_7_), channel_id=1, source_target_pairs={{0,16},{16,0},{1,17},{17,1},{2,18},{18,2},{3,19},{19,3},{4,20},{20... | collective-permute-start | bytes 1990664 | tf_op jit(solution)/shard_map/ppermute | solution.py:174
  54.8 8.7 %collective-permute-start.14 = (f32[9,48,384]{2,1,0:T(8,128)S(1)}, f32[9,48,384]{2,1,0:T(8,128)S(1)}, u32[]{:S(2)}, u32[]{:S(2)}) collective-permute-start(f32[9,48,384]{2,1,0:T(8,128)S(1)} %collective-permute-done.11.refs_1_), channel_id=1, source_target_pairs={{0,4},{4,0},{8,12},{12,8},{1,5},{5,1},{9,13},{13,9},{2,6},{6,2},{1... | collective-permute-start | bytes 1990664 | tf_op jit(solution)/shard_map/ppermute | solution.py:174
  57.0 19.2 %copy-start.15 = (f32[3,128,384]{2,1,0:T(8,128)}, f32[3,128,384]{2,1,0:T(8,128)S(1)}, u32[]{:S(2)}) copy-start(f32[3,128,384]{2,1,0:T(8,128)S(1)} %collective-permute-done.4.refs_4_) | copy-start | bytes 1769476
  57.0 16.6 %collective-permute-start.12 = (f32[9,48,384]{2,1,0:T(8,128)S(1)}, f32[9,48,384]{2,1,0:T(8,128)}, u32[]{:S(2)}, u32[]{:S(2)}) collective-permute-start(f32[9,48,384]{2,1,0:T(8,128)S(1)} %collective-permute-done.11.refs_1_), channel_id=1, source_target_pairs={{0,16},{16,0},{1,17},{17,1},{2,18},{18,2},{3,19},{19,3},{4,20},{20... | collective-permute-start | bytes 1990664 | tf_op jit(solution)/shard_map/ppermute | solution.py:174
  57.2 18.9 %copy-start.16 = (f32[3,128,384]{2,1,0:T(8,128)}, f32[3,128,384]{2,1,0:T(8,128)S(1)}, u32[]{:S(2)}) copy-start(f32[3,128,384]{2,1,0:T(8,128)S(1)} %collective-permute-done.1.refs_1_) | copy-start | bytes 1769476
  57.3 17.2 %collective-permute-start.5 = (f32[3,128,384]{2,1,0:T(8,128)S(1)}, f32[3,128,384]{2,1,0:T(8,128)S(1)}, u32[]{:S(2)}, u32[]{:S(2)}) collective-permute-start(f32[3,128,384]{2,1,0:T(8,128)S(1)} %collective-permute-done.4.refs_4_), channel_id=1, source_target_pairs={{1,0},{2,1},{3,2},{5,4},{6,5},{7,6},{9,8},{10,9},{11,10},{13,12},{... | collective-permute-start | bytes 1769480 | tf_op jit(solution)/shard_map/ppermute | solution.py:219
  60.0 14.4 %copy-start.7 = (f32[9,48,384]{2,1,0:T(8,128)}, f32[9,48,384]{2,1,0:T(8,128)S(1)}, u32[]{:S(2)}) copy-start(f32[9,48,384]{2,1,0:T(8,128)S(1)} %collective-permute-done.19.refs_10_) | copy-start | bytes 1990660
  60.0 16.1 %collective-permute-start.2 = (f32[3,128,384]{2,1,0:T(8,128)S(1)}, f32[3,128,384]{2,1,0:T(8,128)S(1)}, u32[]{:S(2)}, u32[]{:S(2)}) collective-permute-start(f32[3,128,384]{2,1,0:T(8,128)S(1)} %collective-permute-done.1.refs_1_), channel_id=1, source_target_pairs={{0,1},{1,2},{2,3},{4,5},{5,6},{6,7},{8,9},{9,10},{10,11},{12,13},{... | collective-permute-start | bytes 1769480 | tf_op jit(solution)/shard_map/ppermute | solution.py:218
  62.6 11.9 %copy-start.8 = (f32[9,48,384]{2,1,0:T(8,128)}, f32[9,48,384]{2,1,0:T(8,128)S(1)}, u32[]{:S(2)}) copy-start(f32[9,48,384]{2,1,0:T(8,128)S(1)} %collective-permute-done.17.refs_8_) | copy-start | bytes 1990660
  62.6 34.9 %collective-permute-start.23 = (f32[9,96,384]{2,1,0:T(8,128)S(1)}, f32[9,96,384]{2,1,0:T(8,128)}, u32[]{:S(2)}, u32[]{:S(2)}) collective-permute-start(f32[9,96,384]{2,1,0:T(8,128)S(1)} %get-tuple-element.6.refs_12_), channel_id=1, source_target_pairs={{0,4},{4,0},{8,12},{12,8},{1,5},{5,1},{9,13},{13,9},{2,6},{6,2},{1... | collective-permute-start | bytes 3981320 | tf_op jit(solution)/shard_map/ppermute | solution.py:174
  63.6 11.3 %copy-start.10 = (f32[9,48,384]{2,1,0:T(8,128)}, f32[9,48,384]{2,1,0:T(8,128)S(1)}, u32[]{:S(2)}) copy-start(f32[9,48,384]{2,1,0:T(8,128)S(1)} %collective-permute-done.14.refs_4_) | copy-start | bytes 1990660
  63.6 34.0 %collective-permute-start.13 = (f32[9,96,384]{2,1,0:T(8,128)S(1)}, f32[9,96,384]{2,1,0:T(8,128)}, u32[]{:S(2)}, u32[]{:S(2)}) collective-permute-start(f32[9,96,384]{2,1,0:T(8,128)S(1)} %get-tuple-element.7.refs_0_), channel_id=1, source_target_pairs={{0,4},{4,0},{8,12},{12,8},{1,5},{5,1},{9,13},{13,9},{2,6},{6,2},{1... | collective-permute-start | bytes 3981320 | tf_op jit(solution)/shard_map/ppermute | solution.py:174
  73.6 24.5 %collective-permute-start.18 = (f32[9,96,384]{2,1,0:T(8,128)}, f32[9,96,384]{2,1,0:T(8,128)}, u32[]{:S(2)}, u32[]{:S(2)}) collective-permute-start(f32[9,96,384]{2,1,0:T(8,128)} %get-tuple-element.8.refs_6_), channel_id=1, source_target_pairs={{0,4},{4,0},{8,12},{12,8},{1,5},{5,1},{9,13},{13,9},{2,6},{6,2},{1... | collective-permute-start | bytes 3981320 | tf_op jit(solution)/shard_map/ppermute | solution.py:174
  74.4 1.7 %copy-start.17 = (f32[3,128,384]{2,1,0:T(8,128)}, f32[3,128,384]{2,1,0:T(8,128)S(1)}, u32[]{:S(2)}) copy-start(f32[3,128,384]{2,1,0:T(8,128)S(1)} %collective-permute-done.5.refs_5_) | copy-start | bytes 1769476
  74.4 17.5 %collective-permute-start.24 = (f32[9,48,384]{2,1,0:T(8,128)}, f32[9,48,384]{2,1,0:T(8,128)}, u32[]{:S(2)}, u32[]{:S(2)}) collective-permute-start(f32[9,48,384]{2,1,0:T(8,128)} %collective-permute-done.21.refs_13_), channel_id=1, source_target_pairs={{0,4},{4,0},{8,12},{12,8},{1,5},{5,1},{9,13},{13,9},{2,6},{6,2},{1... | collective-permute-start | bytes 1990664 | tf_op jit(solution)/shard_map/ppermute | solution.py:174
  76.2 0.8 copy-start.18
  77.0 17.8 %collective-permute-start.22 = (f32[9,48,384]{2,1,0:T(8,128)}, f32[9,48,384]{2,1,0:T(8,128)}, u32[]{:S(2)}, u32[]{:S(2)}) collective-permute-start(f32[9,48,384]{2,1,0:T(8,128)} %collective-permute-done.21.refs_13_), channel_id=1, source_target_pairs={{0,16},{16,0},{1,17},{17,1},{2,18},{18,2},{3,19},{19,3},{4,20},{20... | collective-permute-start | bytes 1990664 | tf_op jit(solution)/shard_map/ppermute | solution.py:174
  79.6 12.4 %copy-start.9 = (f32[9,48,384]{2,1,0:T(8,128)S(1)}, f32[9,48,384]{2,1,0:T(8,128)}, u32[]{:S(2)}) copy-start(f32[9,48,384]{2,1,0:T(8,128)} %copy-done.8) | copy-start | bytes 1990660
  90.1 17.7 %copy-start.2 = (f32[3,128,384]{2,1,0:T(8,128)S(1)}, f32[3,128,384]{2,1,0:T(8,128)}, u32[]{:S(2)}) copy-start(f32[3,128,384]{2,1,0:T(8,128)} %get-tuple-element.5) | copy-start | bytes 1769476
  92.0 22.9 %collective-permute-start.20 = (f32[9,48,384]{2,1,0:T(8,128)S(1)}, f32[9,48,384]{2,1,0:T(8,128)S(1)}, u32[]{:S(2)}, u32[]{:S(2)}) collective-permute-start(f32[9,48,384]{2,1,0:T(8,128)S(1)} %copy-done.9), channel_id=1, source_target_pairs={{0,4},{4,0},{8,12},{12,8},{1,5},{5,1},{9,13},{13,9},{2,6},{6,2},{1... | collective-permute-start | bytes 1990664 | tf_op jit(solution)/shard_map/ppermute | solution.py:174
  94.8 8.8 %collective-permute-start.10 = (f32[2,1,64,384]{3,2,1,0:T(8,128)S(1)}, f32[2,1,64,384]{3,2,1,0:T(8,128)S(1)}, u32[]{:S(2)}, u32[]{:S(2)}) collective-permute-start(f32[2,1,64,384]{3,2,1,0:T(8,128)S(1)} %get-tuple-element.11), channel_id=1, source_target_pairs={{1,4},{2,5},{3,6},{5,8},{6,9},{7,10},{9,12},{10,13},{11,14},{17,20... | collective-permute-start | bytes 589832 | tf_op jit(solution)/shard_map/ppermute | solution.py:232
  97.5 21.4 %collective-permute-start.15 = (f32[9,48,384]{2,1,0:T(8,128)}, f32[9,48,384]{2,1,0:T(8,128)S(1)}, u32[]{:S(2)}, u32[]{:S(2)}) collective-permute-start(f32[9,48,384]{2,1,0:T(8,128)} %collective-permute-done.12.refs_2_), channel_id=1, source_target_pairs={{0,4},{4,0},{8,12},{12,8},{1,5},{5,1},{9,13},{13,9},{2,6},{6,2},{1... | collective-permute-start | bytes 1990664 | tf_op jit(solution)/shard_map/ppermute | solution.py:174
  97.6 21.3 %collective-permute-start.25 = (f32[9,48,384]{2,1,0:T(8,128)}, f32[9,48,384]{2,1,0:T(8,128)S(1)}, u32[]{:S(2)}, u32[]{:S(2)}) collective-permute-start(f32[9,48,384]{2,1,0:T(8,128)} %collective-permute-done.22.refs_14_), channel_id=1, source_target_pairs={{0,4},{4,0},{8,12},{12,8},{1,5},{5,1},{9,13},{13,9},{2,6},{6,2},{1... | collective-permute-start | bytes 1990664 | tf_op jit(solution)/shard_map/ppermute | solution.py:174
  98.1 28.2 %collective-permute-start.8 = (f32[2,2,64,384]{3,2,1,0:T(8,128)}, f32[2,2,64,384]{3,2,1,0:T(8,128)S(1)}, u32[]{:S(2)}, u32[]{:S(2)}) collective-permute-start(f32[2,2,64,384]{3,2,1,0:T(8,128)} %bitcast.10), channel_id=1, source_target_pairs={{0,4},{1,5},{2,6},{3,7},{4,8},{5,9},{6,10},{7,11},{8,12},{9,13},{1... | collective-permute-start | bytes 1179656 | tf_op jit(solution)/shard_map/ppermute | solution.py:232
  103.6 22.6 %copy-start.22 = (f32[2,1,64,384]{3,2,1,0:T(8,128)}, f32[2,1,64,384]{3,2,1,0:T(8,128)S(1)}, u32[]{:S(2)}) copy-start(f32[2,1,64,384]{3,2,1,0:T(8,128)S(1)} %collective-permute-done.10.past_down) | copy-start | bytes 589828
  103.6 7.8 %collective-permute-start.9 = (f32[2,1,64,384]{3,2,1,0:T(8,128)S(1)}, f32[2,1,64,384]{3,2,1,0:T(8,128)S(1)}, u32[]{:S(2)}, u32[]{:S(2)}) collective-permute-start(f32[2,1,64,384]{3,2,1,0:T(8,128)S(1)} %get-tuple-element.12), channel_id=1, source_target_pairs={{0,5},{1,6},{2,7},{4,9},{5,10},{6,11},{8,13},{9,14},{10,15},{16,21... | collective-permute-start | bytes 589832 | tf_op jit(solution)/shard_map/ppermute | solution.py:232
  111.4 0.7 copy-start.23
  112.1 10.3 %collective-permute-start.7 = (f32[3,1,64,384]{3,2,1,0:T(8,128)S(1)}, f32[3,1,64,384]{3,2,1,0:T(8,128)S(1)}, u32[]{:S(2)}, u32[]{:S(2)}) collective-permute-start(f32[3,1,64,384]{3,2,1,0:T(8,128)S(1)} %get-tuple-element.9), channel_id=1, source_target_pairs={{1,0},{2,1},{3,2},{5,4},{6,5},{7,6},{9,8},{10,9},{11,10},{13,12},{... | collective-permute-start | bytes 884744 | tf_op jit(solution)/shard_map/ppermute | solution.py:232
  114.9 0.8 copy-start.11
  115.7 10.5 %collective-permute-start.6 = (f32[3,1,64,384]{3,2,1,0:T(8,128)S(1)}, f32[3,1,64,384]{3,2,1,0:T(8,128)S(1)}, u32[]{:S(2)}, u32[]{:S(2)}) collective-permute-start(f32[3,1,64,384]{3,2,1,0:T(8,128)S(1)} %get-tuple-element.10), channel_id=1, source_target_pairs={{0,1},{1,2},{2,3},{4,5},{5,6},{6,7},{8,9},{9,10},{10,11},{12,13},{... | collective-permute-start | bytes 884744 | tf_op jit(solution)/shard_map/ppermute | solution.py:232
  118.8 7.4 %copy-start.12 = (f32[9,48,384]{2,1,0:T(8,128)}, f32[9,48,384]{2,1,0:T(8,128)S(1)}, u32[]{:S(2)}) copy-start(f32[9,48,384]{2,1,0:T(8,128)S(1)} %collective-permute-done.15.refs_5_) | copy-start | bytes 1990660
  118.9 7.4 %copy-start.13 = (f32[9,48,384]{2,1,0:T(8,128)}, f32[9,48,384]{2,1,0:T(8,128)S(1)}, u32[]{:S(2)}) copy-start(f32[9,48,384]{2,1,0:T(8,128)S(1)} %collective-permute-done.25.refs_17_) | copy-start | bytes 1990660
  122.4 3.9 %copy-start.20 = (f32[3,1,64,384]{3,2,1,0:T(8,128)}, f32[3,1,64,384]{3,2,1,0:T(8,128)S(1)}, u32[]{:S(2)}) copy-start(f32[3,1,64,384]{3,2,1,0:T(8,128)S(1)} %collective-permute-done.7.down) | copy-start | bytes 884740
  126.2 0.7 copy-start.21
  126.9 0.7 copy-start.19

commit v2 on v0

v2 whole, which is shorter than its diff:
```python
import functools
import math

import jax
import jax.numpy as jnp
from jax import lax
from jax.experimental import pallas as pl
from jax.experimental.pallas import tpu as pltpu
from jax.sharding import PartitionSpec as P

F32, BF16 = jnp.float32, jnp.bfloat16
VMEM_LIMIT = 56 * 1024 * 1024
CHUNKS = 3


def split(x):
    high = x.astype(BF16)
    return high, (x - high.astype(F32)).astype(BF16)


def dot3(a, b, dims=(((1,), (0,)), ((), ()))):
    dot = functools.partial(lax.dot_general, dimension_numbers=dims, preferred_element_type=F32)
    (ah, al), (bh, bl) = a, b
    return dot(ah, bh) + (dot(ah, bl) + dot(al, bh))


TRANSPOSED = (((1,), (1,)), ((), ()))


def rms(v, gain):
    return v * lax.rsqrt(jnp.mean(v * v, axis=-1, keepdims=True) + 1e-06) * gain


MESH = pl.DeviceIdType.MESH


def shard_plan(shards, halved):
    plan, held = [], [(0, 0, None)]
    bit = 1
    while 2 * bit < shards:
        bit *= 2
    while bit >= 1 and shards > 1:
        arrived = []
        for mask, part, source in held:
            if halved and bit > 1 and part == 0:
                plan.append(("tm", bit, mask, 1, source))
                plan.append(("groups", 1, mask ^ bit, 1, len(plan) - 1))
                arrived += [(mask ^ bit, 1, len(plan) - 2), (mask ^ bit, 2, len(plan) - 1)]
            else:
                plan.append(("tm", bit, mask, part, source))
                arrived.append((mask ^ bit, part, len(plan) - 1))
        held += arrived
        bit //= 2
    return plan


def kernel(
    plan, times, tiles, act, gain_a, wq, wk, wv, wo, gain_c, kernel_hbm, attended, out,
    others, hid, up, down, past, past_up, past_down, weights, xh, xl,
    line_send, line_recv, edge_send, edge_recv, shard_send, shard_recv, own_sem,
):
    frames, rows, width, channels = hid.shape
    tokens = rows * width
    group, me, tile = lax.axis_index("groups"), lax.axis_index("tm"), lax.axis_index("tile")
    size = kernel_hbm.shape[1]
    half = size // 2

    barrier = pltpu.get_barrier_semaphore()
    friends = [(True, {"groups": 1 - group})]
    bit = 1
    while bit < times:
        friends.append((True, {"tm": me + bit * (1 - 2 * ((me // bit) % 2))}))
        bit *= 2
    for dt, dz in ((0, 1), (1, 0), (1, 1), (1, -1)):
        for sign in (1, -1):
            t, z = me + sign * dt, tile + sign * dz
            inside = (t >= 0) & (t < times) & (z >= 0) & (z < tiles)
            friends.append((inside, {"tm": t, "tile": z}))
    count = 0
    for inside, device in friends:
        if inside is True:
            pl.semaphore_signal(barrier, inc=1, device_id=device, device_id_type=MESH)
            count = count + 1
        else:

            @pl.when(inside)
            def _(device=device):
                pl.semaphore_signal(barrier, inc=1, device_id=device, device_id_type=MESH)

            count = count + inside.astype(jnp.int32)
    pl.semaphore_wait(barrier, count)

    def copy(src, dst, send, recv, device):
        return pltpu.make_async_remote_copy(
            src_ref=src, dst_ref=dst, send_sem=send, recv_sem=recv, device_id=device, device_id_type=MESH
        )

    def line(f, distance, direction):
        slot_here = distance - 1 if direction > 0 else tiles - distance + 1
        slot_there = distance if direction > 0 else tiles - distance
        src = act.at[f] if distance == 1 else others.at[f, slot_here - 1]
        side = 0 if direction > 0 else 1
        return copy(
            src, others.at[f, slot_there - 1], line_send.at[f, side, distance - 1],
            line_recv.at[f, slot_there - 1], {"tile": tile + direction},
        )

    def sends(distance, direction):
        if direction > 0:
            return (tile >= distance - 1) & (tile < tiles - 1)
        return (tile + distance - 1 <= tiles - 1) & (tile > 0)

    def flip(value, bit):
        return value + bit * (1 - 2 * ((value // bit) % 2))

    def flipped(mask):
        value, bit = me, 1
        while bit <= mask:
            if mask & bit:
                value = flip(value, bit)
            bit *= 2
        return value

    def region(ref, chunk, shard, part, swap, local=False):
        first = group if not swap else 1 - group
        start = {0: 0, 1: first * half, 2: (1 - first) * half}[part]
        row = start if local else shard * size + start
        length = size if part == 0 else half
        if not isinstance(row, int):
            row = pl.multiple_of(row, math.gcd(size, length))
        return ref.at[pl.ds(9 * chunk, 9), pl.ds(row, length)]

    def shard_copy(chunk, k):
        axis, bit, mask, part, source = plan[k]
        there = region(weights, chunk, flipped(mask), part, False)
        src = region(kernel_hbm, chunk, 0, part, False, True) if mask == 0 else there
        device = {"tm": flip(me, bit)} if axis == "tm" else {"groups": 1 - group}
        return copy(src, there, shard_send.at[chunk, k], shard_recv.at[chunk, k], device)

    def shard_arrival(chunk, k):
        axis, bit, mask, part, source = plan[k]
        if axis == "tm":
            here, device = region(weights, chunk, flipped(mask ^ bit), part, False), {"tm": flip(me, bit)}
        else:
            here, device = region(weights, chunk, flipped(mask), part, True), {"groups": 1 - group}
        return copy(here, here, shard_send.at[chunk, k], shard_recv.at[chunk, k], device)

    waited = set()

    def arrive(chunk, k):
        if (chunk, k) in waited:
            return
        waited.add((chunk, k))
        shard_arrival(chunk, k).wait_recv()
        for j, step in enumerate(plan):
            if step[4] == k:
                shard_copy(chunk, j).start()

    early = [k for k, step in enumerate(plan) if step[4] is None and any(s[4] == k for s in plan)]
    later = [k for k, step in enumerate(plan) if step[4] is not None and any(s[4] == k for s in plan)]

    for f in range(frames):
        for direction in (1, -1):

            @pl.when(sends(1, direction))
            def _(f=f, direction=direction):
                line(f, 1, direction).start()

    for chunk in range(CHUNKS):
        for k, step in enumerate(plan):
            if step[4] is None:
                shard_copy(chunk, k).start()
    own_rows = weights.at[:, pl.ds(pl.multiple_of(me * size, size), size)]
    own_copy = pltpu.make_async_copy(kernel_hbm, own_rows, own_sem)
    own_copy.start()

    gain = gain_a[...]
    scale = 1.0 / math.sqrt(channels)
    edges = []

    def edge(number, src, dst, dt, dz):
        t, z = me + dt, tile + dz
        goes = (t < times) & (z >= 0) & (z < tiles)
        comes = (me - dt >= 0) & (tile - dz >= 0) & (tile - dz < tiles)
        move = copy(src, dst, edge_send.at[number], edge_recv.at[number], {"tm": t, "tile": z})

        @pl.when(goes)
        def _():
            move.start()

        edges.append((goes, comes, move, dst))

    for f in range(frames):
        for distance in range(1, tiles):
            for direction in (1, -1):
                comes = tile >= distance if direction > 0 else tile + distance < tiles

                @pl.when(comes)
                def _(f=f, distance=distance, direction=direction):
                    slot = distance if direction > 0 else tiles - distance
                    here = others.at[f, slot - 1]
                    side = 0 if direction > 0 else 1
                    copy(
                        here, here, line_send.at[f, side, distance - 1], line_recv.at[f, slot - 1],
                        {"tile": tile - direction},
                    ).wait_recv()

                if distance + 1 < tiles:

                    @pl.when(sends(distance + 1, direction))
                    def _(f=f, distance=distance, direction=direction):
                        line(f, distance + 1, direction).start()

        if f < CHUNKS and f < frames - 1:
            for k in early:
                arrive(f, k)
        x = act[f]
        normed = split(rms(x, gain))
        queries = dot3(normed, split(wq[...]))
        folded = split(dot3(split(queries), split(wk[...]), TRANSPOSED))
        cells = [normed] + [split(rms(others[f, s], gain)) for s in range(tiles - 1)]
        keys = tuple(jnp.concatenate([c[i] for c in cells], axis=0) for i in range(2))
        scores = dot3(folded, keys, TRANSPOSED) * scale
        powers = jnp.exp(scores - jnp.max(scores, axis=-1, keepdims=True))
        summed = jnp.sum(powers, axis=-1, keepdims=True)
        gathered = dot3(split(powers), keys) / summed
        mixed = dot3(split(gathered), split(wv[...]))
        result = x + dot3(split(mixed), split(wo[...]))
        attended[f] = result
        v = rms(result, gain_c[...])
        hid[f] = (v / (1.0 + jnp.exp(-v))).reshape(rows, width, channels)
        base = 5 * f
        edge(base, hid.at[f, rows - 1], up.at[f], 0, 1)
        edge(base + 1, hid.at[f, 0], down.at[f], 0, -1)
        if f >= frames - 2:
            p = f - (frames - 2)
            edge(base + 2, hid.at[f], past.at[p], 1, 0)
            edge(base + 3, hid.at[f, rows - 1], past_up.at[p], 1, 1)
            edge(base + 4, hid.at[f, 0], past_down.at[p], 1, -1)
        if f < CHUNKS and f < frames - 1:
            for k in later:
                arrive(f, k)

    for chunk in range(CHUNKS):
        for k in early:
            arrive(chunk, k)
    for goes, comes, move, dst in edges:

        @pl.when(comes)
        def _(move=move):
            move.wait_recv()

        @pl.when(jnp.logical_not(comes))
        def _(dst=dst):
            dst[...] = jnp.zeros(dst.shape, F32)

    cell = lax.broadcasted_iota(jnp.int32, (width, channels), 0)
    for f in range(frames + 2):
        for r in range(rows + 2):
            upper, middle, lower, t = (past_up, past, past_down, f) if f < 2 else (up, hid, down, f - 2)
            value = upper[t] if r == 0 else lower[t] if r == rows + 1 else middle[t, r - 1]
            before = jnp.where(cell == 0, 0.0, pltpu.roll(value, 1, 0))
            after = jnp.where(cell == width - 1, 0.0, pltpu.roll(value, width - 1, 0))
            for c, v in enumerate((before, value, after)):
                high, low = split(v)
                xh[f, r, :, c * channels : (c + 1) * channels] = high
                xl[f, r, :, c * channels : (c + 1) * channels] = low
    for chunk in range(CHUNKS):
        for k in later:
            arrive(chunk, k)
    own_copy.wait()
    pixels = frames * tokens
    for a in range(CHUNKS):
        for k in range(len(plan)):
            arrive(a, k)

        def row_taps(b, carry, a=a):
            block = weights[pl.ds(9 * a + 3 * b, 3)].reshape(3 * channels, channels)
            high = xh[pl.ds(a, frames), pl.ds(b, rows)].reshape(pixels, 3 * channels)
            low = xl[pl.ds(a, frames), pl.ds(b, rows)].reshape(pixels, 3 * channels)
            product = dot3((high, low), split(block))
            out[...] = out[...] + product
            return carry

        if a == 0:
            out[...] = jnp.zeros(out.shape, F32)
        lax.fori_loop(0, 3, row_taps, 0)

    for f in range(frames):
        for distance in range(1, tiles):
            for direction in (1, -1):

                @pl.when(sends(distance, direction))
                def _(f=f, distance=distance, direction=direction):
                    line(f, distance, direction).wait_send()

    for goes, comes, move, dst in edges:

        @pl.when(goes)
        def _(move=move):
            move.wait_send()

    for chunk in range(CHUNKS):
        for k in range(len(plan)):
            shard_copy(chunk, k).wait_send()


def body(activations, gain_attention, w_query, w_key, w_value, w_out, gain_conv, conv_weight):
    frames, rows, width, channels = activations.shape
    tokens = rows * width
    own = activations.reshape(frames, tokens, channels)
    times, tiles = lax.axis_size("tm"), lax.axis_size("tile")
    taps, size = conv_weight.shape[:2]
    plan = shard_plan(times, lax.axis_size("groups") == 2 and size % 16 == 0)
    vmem = pl.BlockSpec(memory_space=pltpu.VMEM)
    dma = pltpu.SemaphoreType.DMA
    attended, conv_out = pl.pallas_call(
        functools.partial(kernel, plan, times, tiles),
        in_specs=[vmem] * 7 + [pl.BlockSpec(memory_space=pl.ANY)],
        out_specs=[vmem, vmem],
        out_shape=[
            jax.ShapeDtypeStruct(own.shape, F32),
            jax.ShapeDtypeStruct((frames * tokens, channels), F32),
        ],
        scratch_shapes=[
            pltpu.VMEM((frames, tiles - 1, tokens, channels), F32),
            pltpu.VMEM((frames, rows, width, channels), F32),
            pltpu.VMEM((frames, width, channels), F32),
            pltpu.VMEM((frames, width, channels), F32),
            pltpu.VMEM((2, rows, width, channels), F32),
            pltpu.VMEM((2, width, channels), F32),
            pltpu.VMEM((2, width, channels), F32),
            pltpu.VMEM((taps, channels, channels), F32),
            pltpu.VMEM((frames + 2, rows + 2, width, 3 * channels), BF16),
            pltpu.VMEM((frames + 2, rows + 2, width, 3 * channels), BF16),
            dma((frames, 2, tiles - 1)),
            dma((frames, tiles - 1)),
            dma((5 * frames,)),
            dma((5 * frames,)),
            dma((CHUNKS, len(plan))),
            dma((CHUNKS, len(plan))),
            dma,
        ],
        compiler_params=pltpu.CompilerParams(
            collective_id=0, has_side_effects=True, vmem_limit_bytes=VMEM_LIMIT
        ),
    )(
        own, gain_attention.reshape(1, -1), w_query, w_key, w_value, w_out, gain_conv.reshape(1, -1), conv_weight
    )
    return (attended.reshape(activations.shape), conv_out.reshape(activations.shape))


def solution(mesh):
    placed = P(("groups", "tm"), "tile", None, None)
    return jax.shard_map(
        body,
        mesh=mesh,
        in_specs=(placed, P(), P(), P(), P(), P(), P(), P(None, "tm", None)),
        out_specs=(placed, placed),
        check_vma=False,
    )
```

time: 257 us -> 112 us (0.44)
  waiting for transfers between devices: 160 us -> 0 us
  Pallas kernels: 0 us -> 105 us
  matrix products: 48.5 us -> 0 us
  local copies, waits for them, and re-layouts: 22 us -> 6.32 us
  between operations: 13.9 us -> 0.64 us
  other arithmetic: 6.63 us -> 0 us
  starting transfers between devices: 5 us -> 0 us
    all_gather x3 -> x0, waiting for transfers between devices: 149 us -> none  [the longest x1 55.2 us: body(): piece = lax.all_gather(conv_weight, 'tm', axis=1, tiled=True)]
    pallas_call x0 -> x1, Pallas kernels: none -> 105 us  [body(): pl.pallas_call(functools.partial(kernel, plan, times, tiles), in_specs=[v...]
    dot_general x7 -> x0, matrix products: 48.5 us -> none  [the longest x1 30.7 us: body(): jnp.dot(columns, piece.reshape(27 * count, channels), precision=highest)]
    unnamed x31 -> x2, local copies, waits for them, and re-layouts: 21 us -> 3.83 us
    ppermute x3 -> x0, waiting for transfers between devices: 10.6 us -> none  [the longest x1 4.82 us: padded_2(): before = lax.ppermute(last, axis, up)]
    ppermute x3 -> x0, starting transfers between devices: 4.88 us -> none  [the longest x1 1.76 us: from_behind(): return lax.ppermute(block, axis, route)]
    unnamed x3 -> x0, other arithmetic: 2.95 us -> none
  transfers between devices with their start and end apart: 6 -> 0, of which waited for: 6 -> 0; matrix products, arithmetic and copies ran while one was open for 16% -> 0% of each run, Pallas kernels for 0% -> 0%
where the time goes in v2:
time: 112 us
  Pallas kernels  105 us (94%)
  local copies, waits for them, and re-layouts  6.32 us (6%)
    pallas_call x1, Pallas kernels, body(): pl.pallas_call(functools.partial(kernel, plan, times, tiles), in_specs=[v...  105 us
    unnamed x2, local copies, waits for them, and re-layouts  3.83 us

profile of v2, /device:TPU:0, one launch (start us, length us, event | category | flops | bytes accessed | tf_op | source)
XLA Modules:
  0.0 111.7 jit_solution(2664028329202272904)
XLA Ops:
  0.6 1.2 %reshape.20.gain_a = f32[1,384]{1,0:T(1,128)} reshape(f32[384]{0:T(512)} %param.9) | data formatting | bytes 3072 | tf_op jit(solution)/shard_map/reshape | solution.py:348
  1.9 1.2 %reshape.21.gain_c = f32[1,384]{1,0:T(1,128)} reshape(f32[384]{0:T(512)} %param.14) | data formatting | bytes 3072 | tf_op jit(solution)/shard_map/reshape | solution.py:348
  3.1 104.7 %shard_map.95 = (f32[3,128,384]{2,1,0:T(8,128)}, f32[384,384]{1,0:T(8,128)}) custom-call(f32[3,128,384]{2,1,0:T(8,128)} %bitcast.5, f32[1,384]{1,0:T(1,128)} %reshape.20.gain_a, f32[384,384]{1,0:T(8,128)} %wq.1, f32[384,384]{1,0:T(8,128)} %wk.1, f32[384,384]{1,0:T(8,128)} %wv.1, f32[384,384]{1,0:T(8,128)} %wo.1, f32[1,384]{1,0:T(1,128)} %reshape.21.gain_c, ...), custom_call_target="tpu_custom_call" | custom-call | tf_op jit(solution)/shard_map/pallas_call | solution.py:317
  107.8 1.9 %copy.12 = f32[3,2,64,384]{3,2,1,0:T(8,128)} copy(f32[3,2,64,384]{3,2,1,0:T(8,128)} %bitcast.4) | data formatting | bytes 1179648
  109.7 1.9 %copy.13 = f32[3,2,64,384]{3,2,1,0:T(8,128)} copy(f32[3,2,64,384]{3,2,1,0:T(8,128)} %bitcast.3) | data formatting | bytes 1179648

commit v3 on v2

--- a/solution.py
+++ b/solution.py
@@ -145,6 +145,9 @@
             here, device = region(weights, chunk, flipped(mask), part, True), {"groups": 1 - group}
         return copy(here, here, shard_send.at[chunk, k], shard_recv.at[chunk, k], device)
 
+    early = [k for k, step in enumerate(plan) if step[4] is None and any(s[4] == k for s in plan)]
+    later = [k for k, step in enumerate(plan) if step[4] is not None and any(s[4] == k for s in plan)]
+
     waited = set()
 
     def arrive(chunk, k):
@@ -152,29 +155,41 @@
             return
         waited.add((chunk, k))
         shard_arrival(chunk, k).wait_recv()
+        if k in early and chunk + 1 < CHUNKS:
+            shard_copy(chunk + 1, k).start()
         for j, step in enumerate(plan):
             if step[4] == k:
                 shard_copy(chunk, j).start()
 
-    early = [k for k, step in enumerate(plan) if step[4] is None and any(s[4] == k for s in plan)]
-    later = [k for k, step in enumerate(plan) if step[4] is not None and any(s[4] == k for s in plan)]
-
-    for f in range(frames):
+    def start_line(f):
         for direction in (1, -1):
 
             @pl.when(sends(1, direction))
-            def _(f=f, direction=direction):
+            def _(direction=direction):
                 line(f, 1, direction).start()
 
+    start_line(0)
     for chunk in range(CHUNKS):
         for k, step in enumerate(plan):
-            if step[4] is None:
+            if step[4] is None and (chunk == 0 or k not in early):
                 shard_copy(chunk, k).start()
     own_rows = weights.at[:, pl.ds(pl.multiple_of(me * size, size), size)]
     own_copy = pltpu.make_async_copy(kernel_hbm, own_rows, own_sem)
     own_copy.start()
 
-    gain = gain_a[...]
+    cell = lax.broadcasted_iota(jnp.int32, (width, channels), 0)
+
+    def place(f, r):
+        upper, middle, lower, t = (past_up, past, past_down, f) if f < 2 else (up, hid, down, f - 2)
+        value = upper[t] if r == 0 else lower[t] if r == rows + 1 else middle[t, r - 1]
+        before = jnp.where(cell == 0, 0.0, pltpu.roll(value, 1, 0))
+        after = jnp.where(cell == width - 1, 0.0, pltpu.roll(value, width - 1, 0))
+        for c, v in enumerate((before, value, after)):
+            high, low = split(v)
+            xh[f, r, :, c * channels : (c + 1) * channels] = high
+            xl[f, r, :, c * channels : (c + 1) * channels] = low
+
+    gain = gain_a[...].reshape(1, channels)
     scale = 1.0 / math.sqrt(channels)
     edges = []
 
@@ -211,6 +226,10 @@
                     def _(f=f, distance=distance, direction=direction):
                         line(f, distance + 1, direction).start()
 
+            if distance == 1 and f + 1 < frames:
+                start_line(f + 1)
+        if tiles == 1 and f + 1 < frames:
+            start_line(f + 1)
         if f < CHUNKS and f < frames - 1:
             for k in early:
                 arrive(f, k)
@@ -227,7 +246,7 @@
         mixed = dot3(split(gathered), split(wv[...]))
         result = x + dot3(split(mixed), split(wo[...]))
         attended[f] = result
-        v = rms(result, gain_c[...])
+        v = rms(result, gain_c[...].reshape(1, channels))
         hid[f] = (v / (1.0 + jnp.exp(-v))).reshape(rows, width, channels)
         base = 5 * f
         edge(base, hid.at[f, rows - 1], up.at[f], 0, 1)
@@ -237,9 +256,11 @@
             edge(base + 2, hid.at[f], past.at[p], 1, 0)
             edge(base + 3, hid.at[f, rows - 1], past_up.at[p], 1, 1)
             edge(base + 4, hid.at[f, 0], past_down.at[p], 1, -1)
-        if f < CHUNKS and f < frames - 1:
+        for r in range(1, rows + 1):
+            place(f + 2, r)
+        if 1 <= f < frames - 1 and f <= CHUNKS:
             for k in later:
-                arrive(f, k)
+                arrive(f - 1, k)
 
     for chunk in range(CHUNKS):
         for k in early:
@@ -254,17 +275,10 @@
         def _(dst=dst):
             dst[...] = jnp.zeros(dst.shape, F32)
 
-    cell = lax.broadcasted_iota(jnp.int32, (width, channels), 0)
     for f in range(frames + 2):
         for r in range(rows + 2):
-            upper, middle, lower, t = (past_up, past, past_down, f) if f < 2 else (up, hid, down, f - 2)
-            value = upper[t] if r == 0 else lower[t] if r == rows + 1 else middle[t, r - 1]
-            before = jnp.where(cell == 0, 0.0, pltpu.roll(value, 1, 0))
-            after = jnp.where(cell == width - 1, 0.0, pltpu.roll(value, width - 1, 0))
-            for c, v in enumerate((before, value, after)):
-                high, low = split(v)
-                xh[f, r, :, c * channels : (c + 1) * channels] = high
-                xl[f, r, :, c * channels : (c + 1) * channels] = low
+            if f < 2 or r in (0, rows + 1):
+                place(f, r)
     for chunk in range(CHUNKS):
         for k in later:
             arrive(chunk, k)
@@ -345,7 +359,7 @@
             collective_id=0, has_side_effects=True, vmem_limit_bytes=VMEM_LIMIT
         ),
     )(
-        own, gain_attention.reshape(1, -1), w_query, w_key, w_value, w_out, gain_conv.reshape(1, -1), conv_weight
+        own, gain_attention, w_query, w_key, w_value, w_out, gain_conv, conv_weight
     )
     return (attended.reshape(activations.shape), conv_out.reshape(activations.shape))
 

time: 112 us -> 95.8 us (0.86)
  Pallas kernels: 105 us -> 90.7 us
  local copies, waits for them, and re-layouts: 6.32 us -> 3.83 us
    pallas_call x1, Pallas kernels: 105 us -> 90.7 us  [body(): pl.pallas_call(functools.partial(kernel, plan, times, tiles), in_specs=[v...]
    reshape x2 -> x0, local copies, waits for them, and re-layouts: 2.49 us -> none  [the longest x1 1.25 us: body(): gain_attention.reshape(1, -1)]
where the time goes in v3:
time: 95.8 us; the launch traced here: 95.1 us
  Pallas kernels  90.7 us (95%)
  local copies, waits for them, and re-layouts  3.83 us (4%)
    pallas_call x1, Pallas kernels, body(): pl.pallas_call(functools.partial(kernel, plan, times, tiles), in_specs=[v...  90.7 us
    unnamed x2, local copies, waits for them, and re-layouts  3.83 us

profile of v3, /device:TPU:0, one launch (start us, length us, event | category | flops | bytes accessed | tf_op | source)
XLA Modules:
  0.0 95.1 jit_solution(6208042350677306929)
XLA Ops:
  0.6 90.7 %shard_map.95 = (f32[3,128,384]{2,1,0:T(8,128)}, f32[384,384]{1,0:T(8,128)}) custom-call(f32[3,128,384]{2,1,0:T(8,128)} %bitcast.3, f32[384]{0:T(512)} %gain_a.1, f32[384,384]{1,0:T(8,128)} %wq.1, f32[384,384]{1,0:T(8,128)} %wk.1, f32[384,384]{1,0:T(8,128)} %wv.1, f32[384,384]{1,0:T(8,128)} %wo.1, f32[384]{0:T(512)} %gain_c.1, f32[27,96,384]{2,1,0:T(8,128)} %kernel_hbm.1), custom_call_target="tpu_custom_call" | custom-call | tf_op jit(solution)/shard_map/pallas_call | solution.py:331
  91.3 1.9 %copy.12 = f32[3,2,64,384]{3,2,1,0:T(8,128)} copy(f32[3,2,64,384]{3,2,1,0:T(8,128)} %bitcast.5) | data formatting | bytes 1179648
  93.2 1.9 %copy.13 = f32[3,2,64,384]{3,2,1,0:T(8,128)} copy(f32[3,2,64,384]{3,2,1,0:T(8,128)} %bitcast.4) | data formatting | bytes 1179648
